TPU v7x, 256 devices: a whole 4x4x8 slice. The times are simulated.
256 devices in a mesh: blk: 16 (over x_hi, z), wide: 16 (over y, x_lo, core).
Axes of the slice: x: 4 (x_hi: 2, x_lo: 2; x = x_hi * 2 + x_lo), y: 4, z: 8, core: 2. Of those that a mesh axis runs over, the one named last changes fastest.
Arguments:
- blocks: bfloat16 [4096, 64, 4096], P(('blk', 'wide')), may hold values from -24 to 24
- block_row: int32 [4096], P(('blk', 'wide')), may hold values from 0 to 3
- block_depth: int32 [4096], P(('blk', 'wide')), may hold values from 0 to 15
- live: int32 [4096], P(('blk', 'wide')), may hold values from 0 to 1, as said below
- factor_b: bfloat16 [1024, 256], P('blk'), may hold values from -6 to 6
- factor_c: bfloat16 [1024, 256], replicated, may hold values from -6 to 6
Outputs:
- factor_a: bfloat16 [4096, 256], P('wide')
- factor_b_new: bfloat16 [1024, 256], P(('blk', 'wide'))
Inputs may be any that keep to these rules, and one draw needn't show every extreme that they name: 1 marks a slot that holds a block, 0 an empty one; the share of live slots differs between devices, and slots 0 to 15 are all live.
All inputs are finite; a program needn't handle non-finite values.
Results may differ from a plain program's by a relative error of at most 0.0091.
Values may be sent and summed in bfloat16 or wider, within the bound.
A program may use at most 64 MiB of HBM per device.

v0:
```python
import jax
import jax.numpy as jnp
from jax import lax
from jax.sharding import PartitionSpec as P

BLOCK = 64
ROW_BLOCKS = 4
ROWS_C = 1024


RIDGE = 0.05


def factor_solve(partial_rows, gram):
    size = gram.shape[0]
    system = gram + RIDGE * jnp.eye(size, dtype=jnp.float32)
    lower = jnp.linalg.cholesky(system)
    solved = jax.scipy.linalg.cho_solve((lower, True), partial_rows.T)
    return solved.T * (0.125 / BLOCK)


def first_term(block, brows, crows):
    width = brows.shape[1]
    paired = (brows.astype(jnp.float32)[:, None, :] * crows.astype(jnp.float32)[None, :, :]).astype(
        jnp.bfloat16
    )
    return jnp.dot(block, paired.reshape(-1, width), preferred_element_type=jnp.float32)


def second_term(block, arows, crows):
    edge = arows.shape[0]
    paired = (arows.astype(jnp.float32)[:, None, :] * crows.astype(jnp.float32)[None, :, :]).astype(
        jnp.bfloat16
    )
    cube = block.reshape(edge, edge, edge)
    return lax.dot_general(
        cube, paired, (((0, 2), (0, 1)), ((), ())), preferred_element_type=jnp.float32
    )


def per_device(blocks, block_row, block_depth, live, factor_b, factor_c):
    edge = blocks.shape[1]
    slot_total = blocks.shape[0]
    rank = factor_c.shape[1]
    slice_rows = ROW_BLOCKS * BLOCK
    weights = live.astype(jnp.float32)
    gram_c = jnp.dot(factor_c.T, factor_c, preferred_element_type=jnp.float32) / ROWS_C
    empty_rows = jnp.zeros((slice_rows, rank), jnp.float32)
    gram_scale = lax.axis_size("blk") * edge
    piece = lax.all_gather(factor_b, "blk", axis=0, tiled=True)
    count = piece.shape[0] // edge

    def one_slot(step, acc):
        brows = lax.dynamic_slice_in_dim(piece, step * edge, edge, 0)
        crows = lax.dynamic_slice_in_dim(factor_c, block_depth[step] * edge, edge, 0)
        term = first_term(blocks[step], brows, crows) * weights[step]
        row = block_row[step] * edge
        current = lax.dynamic_slice_in_dim(acc, row, edge, 0)
        return lax.dynamic_update_slice_in_dim(acc, current + term, row, 0)

    mttkrp_part = lax.fori_loop(0, count, one_slot, empty_rows)
    panel_gram = jnp.dot(factor_b.T, factor_b, preferred_element_type=jnp.float32)
    gram_b = lax.psum(panel_gram, "blk") / gram_scale
    system_a = gram_c * gram_b
    total_rows = lax.axis_size("wide") * slice_rows
    mttkrp_a = lax.psum(mttkrp_part, "blk")
    factor_a = factor_solve(mttkrp_a, system_a).astype(jnp.bfloat16)
    slice_gram = jnp.dot(factor_a.T, factor_a, preferred_element_type=jnp.float32)
    gram_a = lax.psum(slice_gram, "wide") / total_rows

    def second_part(slot):
        arows = lax.dynamic_slice_in_dim(factor_a, block_row[slot] * edge, edge, 0)
        crows = lax.dynamic_slice_in_dim(factor_c, block_depth[slot] * edge, edge, 0)
        return second_term(blocks[slot], arows, crows) * weights[slot]

    partials = lax.map(second_part, jnp.arange(slot_total, dtype=jnp.int32))
    flat = partials.reshape(slot_total * edge, rank)
    mttkrp_b = lax.psum_scatter(flat, ("blk", "wide"), scatter_dimension=0, tiled=True)
    factor_b_new = factor_solve(mttkrp_b, gram_c * gram_a).astype(jnp.bfloat16)
    return (factor_a, factor_b_new)


def solution(mesh):
    in_specs = (
        P(("blk", "wide"), None, None),
        P(("blk", "wide")),
        P(("blk", "wide")),
        P(("blk", "wide")),
        P("blk", None),
        P(),
    )
    out_specs = (P("wide", None), P(("blk", "wide"), None))
    return jax.shard_map(
        per_device, mesh=mesh, in_specs=in_specs, out_specs=out_specs, check_vma=False
    )
```

profile of v0, /device:TPU:1, one launch (start us, length us, event | category | flops | bytes accessed | tf_op | source)
XLA Modules:
  0.0 851.2 jit_solution(16122719357660556276)
XLA Ops:
  7.2 40.7 %all_gather.3 = bf16[1024,256]{1,0:T(8,128)(2,1)S(1)} all-gather(bf16[64,256]{1,0:T(8,128)(2,1)} %param.15), channel_id=1, replica_groups=mesh['blk'=16,'wide'=16] {'blk'}, dimensions={0}, use_global_device_ids=true | all-gather | bytes 557056 | tf_op jit(solution)/shard_map/all_gather | solution.py:50
  47.9 1.8 fusion.44
  50.4 134.5 %while.25 = (s32[]{:T(128)}, f32[256,256]{1,0:T(8,128)S(1)}, s32[16]{0:T(128)}, bf16[16,64,4096]{2,1,0:T(8,128)(2,1)}, bf16[1024,256]{1,0:T(8,128)(2,1)S(1)}, /*...) while((s32[]{:T(128)}, f32[256,256]{1,0:T(8,128)S(1)}, ...), condition=%wide.region_6.8_spmd, body=%wide.region_5.7_spmd.sunk | while | flops 136380432 | bytes 5178687 | solution.py:61
  53.9 1.3 dynamic_slice.96
  56.6 2.2 fusion.74
  62.3 1.3 dynamic_slice.96
  65.0 2.2 fusion.74
  70.7 1.3 dynamic_slice.96
  73.4 2.2 fusion.74
  79.1 1.3 dynamic_slice.96
  81.8 2.2 fusion.74
  87.5 1.3 dynamic_slice.96
  90.2 2.2 fusion.74
  95.9 1.3 dynamic_slice.96
  98.6 2.2 fusion.74
  104.3 1.3 dynamic_slice.96
  107.0 2.2 fusion.74
  112.7 1.3 dynamic_slice.96
  115.4 2.2 fusion.74
  121.1 1.3 dynamic_slice.96
  123.8 2.2 fusion.74
  129.5 1.3 dynamic_slice.96
  132.2 2.2 fusion.74
  140.6 2.2 fusion.74
  149.1 2.2 fusion.74
  157.5 2.2 fusion.74
  163.2 1.3 dynamic_slice.96
  165.9 2.2 fusion.74
  171.6 1.3 dynamic_slice.96
  174.3 2.2 fusion.74
  180.0 1.3 dynamic_slice.96
  182.7 2.2 fusion.74
  185.7 148.1 %all-reduce.11.cloned.1.call-done = (f32[256,256]{0,1:T(8,128)}, f32[256,256]{0,1:T(8,128)}) async-done(((f32[256,256]{0,1:T(8,128)}, f32[256,256]{0,1:T(8,128)}), (f32[256,256]{0,1:T(8,128)}, f32[256,256]{0,1:T(8,128)})) %all-reduce.11.cloned.1.call-update) | async-done | bytes 524304 | tf_op jit(solution)/shard_map/psum | solution.py:66
  333.8 1.8 select_add_fusion.1
  335.8 11.7 %cholesky.130 = f32[128,128]{1,0:T(8,128)S(1)} custom-call(f32[128,128]{1,0:T(8,128)S(1)} %cholesky.194), custom_call_target="Cholesky" | custom-call | tf_op jit(solution)/shard_map/jit(cholesky)/cholesky | solution.py:17
  347.6 9.8 %custom-call.25 = f32[1,128,128]{1,2,0:T(8,128)S(1)} custom-call(f32[1,128,128]{2,1,0:T(8,128)S(1)} %get-tuple-element.324), custom_call_target="InvertDiagBlocksLowerTriangular" | custom-call | tf_op jit(solution)/shard_map/jit(cholesky)/cholesky | solution.py:17
  357.9 11.7 %cholesky.147 = f32[128,128]{1,0:T(8,128)S(1)} custom-call(f32[128,128]{1,0:T(8,128)S(1)} %convolution_subtract_fusion.3), custom_call_target="Cholesky" | custom-call | tf_op jit(solution)/shard_map/jit(cholesky)/cholesky | solution.py:17
  372.0 4.4 while.27
  372.9 1.3 dynamic-slice.15
  375.0 1.3 dynamic-slice.15
  376.5 19.7 %custom-call.22 = f32[2,128,128]{1,2,0:T(8,128)S(1)} custom-call(f32[2,128,128]{2,1,0:T(8,128)S(1)} %get-tuple-element.198), custom_call_target="InvertDiagBlocksLowerTriangular" | custom-call | tf_op jit(solution)/shard_map/jit(_cho_solve)/triangular_solve | solution.py:18
  399.1 175.9 %while.26 = (s32[]{:T(128)}, f32[16,64,256]{2,1,0:T(8,128)}, s32[16]{0:T(128)S(1)}, bf16[16,64,4096]{2,1,0:T(8,128)(2,1)}, s32[16]{0:T(128)S(1)}, /*index=5*/bf1...) while((s32[]{:T(128)}, f32[16,64,256]{2,1,0:T(8,128)}, ...), condition=%wide.region_10.12_spmd, body=%wide.region_9.11_spmd.sunk | while | flops 136364048 | bytes 3016007 | solution.py:76
  408.3 1.9 fusion.76
  419.3 1.9 fusion.76
  430.3 1.9 fusion.76
  441.3 1.9 fusion.76
  452.3 1.9 fusion.76
  463.3 1.9 fusion.76
  474.3 1.9 fusion.76
  485.3 1.9 fusion.76
  496.3 1.9 fusion.76
  507.3 1.9 fusion.76
  518.3 1.9 fusion.76
  529.2 1.9 fusion.76
  540.2 1.9 fusion.76
  551.2 1.9 fusion.76
  562.2 1.9 fusion.76
  573.2 1.9 fusion.76
  576.3 11.7 %cholesky.164 = f32[128,128]{1,0:T(8,128)S(1)} custom-call(f32[128,128]{1,0:T(8,128)S(1)} %cholesky.197), custom_call_target="Cholesky" | custom-call | tf_op jit(solution)/shard_map/jit(cholesky)/cholesky | solution.py:17
  588.1 9.8 %custom-call.26 = f32[1,128,128]{1,2,0:T(8,128)S(1)} custom-call(f32[1,128,128]{2,1,0:T(8,128)S(1)} %get-tuple-element.322), custom_call_target="InvertDiagBlocksLowerTriangular" | custom-call | tf_op jit(solution)/shard_map/jit(cholesky)/cholesky | solution.py:17
  598.4 11.7 %cholesky.181 = f32[128,128]{1,0:T(8,128)S(1)} custom-call(f32[128,128]{1,0:T(8,128)S(1)} %convolution_subtract_fusion.2), custom_call_target="Cholesky" | custom-call | tf_op jit(solution)/shard_map/jit(cholesky)/cholesky | solution.py:17
  613.1 4.3 while.28
  617.4 19.7 %custom-call.23 = f32[2,128,128]{1,2,0:T(8,128)S(1)} custom-call(f32[2,128,128]{2,1,0:T(8,128)S(1)} %get-tuple-element.206), custom_call_target="InvertDiagBlocksLowerTriangular" | custom-call | tf_op jit(solution)/shard_map/jit(_cho_solve)/triangular_solve | solution.py:18
  637.1 204.9 %all-reduce.9.cloned.1.call-done = f32[1024,256]{1,0:T(8,128)} async-done(((f32[1024,256]{1,0:T(8,128)}), f32[1024,256]{1,0:T(8,128)}) %all-reduce.9.cloned.1.call-update) | async-done | bytes 1048592
  (271 shorter events, 167.2 us)
Async XLA Ops:
  7.2 326.6 %all-reduce.11.cloned.1.call-start = ((), (), s32[]{:S(2)}) async-start(), calls=%async_computation.2 | async-start | bytes 1048576 | tf_op jit(solution)/shard_map/psum | solution.py:66
  184.9 0.7 copy-start
  185.6 389.5 %all-reduce.7.cloned.1.call-start = ((), (), s32[]{:S(2)}) async-start(), calls=%async_computation | async-start | bytes 524288 | tf_op jit(solution)/shard_map/psum | solution.py:69
  333.8 62.3 %copy-start.2 = (f32[256,256]{0,1:T(8,128)S(1)}, f32[256,256]{0,1:T(8,128)}, u32[]{:S(2)}) copy-start(f32[256,256]{0,1:T(8,128)} %get-tuple-element.311) | copy-start | bytes 786436
  335.8 63.3 %copy-start.3 = (s32[16]{0:T(128)S(1)}, s32[16]{0:T(128)}, u32[]{:S(2)}) copy-start(s32[16]{0:T(128)} %get-tuple-element.639) | copy-start | bytes 196
  335.8 63.3 %copy-start.4 = (s32[16]{0:T(128)S(1)}, s32[16]{0:T(128)}, u32[]{:S(2)}) copy-start(s32[16]{0:T(128)} %get-tuple-element.640) | copy-start | bytes 196
  399.0 443.0 %all-reduce.9.cloned.1.call-start = ((), (), s32[]{:S(2)}) async-start(), calls=%async_computation.1 | async-start | bytes 2097152
  575.1 269.5 %copy-start.1 = (bf16[256,256]{1,0:T(8,128)(2,1)}, bf16[256,256]{1,0:T(8,128)(2,1)S(1)}, u32[]{:S(2)}) copy-start(bf16[256,256]{1,0:T(8,128)(2,1)S(1)} %get-tuple-element.633) | copy-start | bytes 393220
Sparse Core Ops, SparseCore 0:
  185.8 148.0 all-reduce.10
  399.1 132.0 all-reduce.6
  575.2 266.7 all-reduce.8
where the time goes:
time: 858 us; the launch traced here: 851 us
  waiting for transfers between devices  353 us (41%)
  other arithmetic  146 us (17%)
  local copies, waits for them, and re-layouts  142 us (17%)
  loops' own time  79.6 us (9%)
  matrix products  73.4 us (9%)
  blocking collectives  40.7 us (5%)
  between operations  16.6 us (2%)
    unnamed x4, waiting for transfers between devices  205 us
    psum x1, waiting for transfers between devices, per_device(): mttkrp_a = lax.psum(mttkrp_part, 'blk')  148 us
    another operation x13, other arithmetic, factor_solve(): lower = jnp.linalg.cholesky(system)  68.6 us
    another operation x1, loops' own time, per_device(): partials = lax.map(second_part, jnp.arange(slot_total, dtype=jnp.int32))  55.9 us
    all_gather x1, blocking collectives, per_device(): piece = lax.all_gather(factor_b, 'blk', axis=0, tiled=True)  40.7 us
    another operation x5, other arithmetic, factor_solve(): solved = jax.scipy.linalg.cho_solve((lower, True), partial_rows.T)  39.4 us
    dot_general x16, matrix products, first_term(): jnp.dot(block, paired.reshape(-1, width), preferred_element_type=jnp.floa...  35.1 us
    dot_general x16, matrix products, second_term(): lax.dot_general(cube, paired, (((0, 2), (0, 1)), ((), ())), preferred_ele...  29.8 us
  transfers between devices with their start and end apart: 3, of which 2 were waited for; matrix products, arithmetic and copies ran while one was open for 21% of the time, Pallas kernels for 0%

commit v1 on v0

v1 whole, which is shorter than its diff:
```python
import functools

import jax
import jax.numpy as jnp
from jax import lax
from jax.experimental import pallas as pl
from jax.experimental.pallas import tpu as pltpu
from jax.sharding import PartitionSpec as P

EDGE = 64
RANK = 256
ROW_BLOCKS = 4
RIDGE = 0.05
SCALE = 0.125 / EDGE
PANEL = 32
F32 = jnp.float32
BF16 = jnp.bfloat16
MESH = pl.DeviceIdType.MESH
TN = (((0,), (0,)), ((), ()))


def split3(x):
    hi = x.astype(BF16)
    rest = x - hi.astype(F32)
    mid = rest.astype(BF16)
    low = (rest - mid.astype(F32)).astype(BF16)
    return hi, mid, low


def small_inverse(cols):
    sub = lax.broadcasted_iota(jnp.int32, (8, 128), 0)
    for k in range(8):
        row = [c[k : k + 1, :] for c in cols]
        inv = 1.0 / jnp.broadcast_to(row[k], (8, 128))
        here = sub == k
        pivot_col = cols[k]
        new = []
        for j in range(8):
            if j == k:
                new.append(jnp.where(here, inv, -pivot_col * inv))
            else:
                scaled = row[j] * inv
                new.append(jnp.where(here, scaled, cols[j] - pivot_col * scaled))
        cols = new
    return cols


def panel_eliminate(groups):
    lane = lax.broadcasted_iota(jnp.int32, (8, RANK), 1)
    count = len(groups)
    for s in range(count):
        base = 8 * s
        cols = [
            jnp.broadcast_to(groups[s][:, base + j : base + j + 1], (8, 128)) for j in range(8)
        ]
        others = {
            g: [jnp.broadcast_to(groups[g][:, base + j : base + j + 1], (8, RANK)) for j in range(8)]
            for g in range(count)
            if g != s
        }
        inv = [jnp.concatenate([c, c], axis=1) for c in small_inverse(cols)]
        terms = [inv[j] * groups[s][j : j + 1, :] for j in range(8)]
        while len(terms) > 1:
            terms = [terms[i] + terms[i + 1] for i in range(0, len(terms), 2)]
        rows = terms[0]
        for j in range(8):
            rows = jnp.where(lane == base + j, inv[j], rows)
        inside = (lane >= base) & (lane < base + 8)
        new = []
        for g in range(count):
            if g == s:
                new.append(rows)
                continue
            kept = jnp.where(inside, 0.0, groups[g])
            parts = [others[g][j] * rows[j : j + 1, :] for j in range(8)]
            while len(parts) > 1:
                parts = [parts[i] + parts[i + 1] for i in range(0, len(parts), 2)]
            new.append(kept - parts[0])
        groups = new
    return groups


def invert_steps(mat, first, last):
    lane = lax.broadcasted_iota(jnp.int32, (1, RANK), 1)

    def step(p, carry):
        r0 = pl.multiple_of(p * PANEL, PANEL)
        panel = mat[pl.ds(r0, PANEL), :]
        rolled = pltpu.roll(panel, lax.rem(RANK - r0, RANK), 1)
        groups = panel_eliminate([rolled[8 * g : 8 * g + 8, :] for g in range(PANEL // 8)])
        rows = pltpu.roll(jnp.concatenate(groups, axis=0), r0, 1)
        before = lane < r0
        inside = (lane >= r0) & (lane < r0 + PANEL)
        sign = jnp.where(before, -1.0, jnp.where(inside, 0.0, 1.0))
        qh, qm, ql = split3(panel * sign)
        wh, wm, wl = split3(rows)
        left = jnp.concatenate([qh, qh, qh, qm, qm, ql], axis=0)
        right = jnp.concatenate([wh, wm, wl, wh, wm, wh], axis=0)
        for half in range(2):
            cut = pl.ds(half * 128, 128)
            update = lax.dot_general(
                left[:, half * 128 : half * 128 + 128], right, TN, preferred_element_type=F32
            )
            mat[cut, :] = jnp.where(inside, 0.0, mat[cut, :]) - update
        mat[pl.ds(r0, PANEL), :] = rows
        return carry

    lax.fori_loop(first, last, step, 0)


def kernel(
    nb,
    nw,
    total_rows,
    block_row,
    block_depth,
    live,
    blocks,
    fb,
    fc,
    out_a,
    out_b,
    x,
    bg,
    acc,
    ra,
    ca,
    fa,
    gram_c,
    mat_a,
    mat_b,
    gl,
    gr,
    gs,
    gfull,
    bd,
    y,
    tf,
    tsend,
    trecv,
    us,
    ur,
    x_sem,
    b_s,
    b_r,
    ra_s,
    ra_r,
    ca_s,
    ca_r,
    g1_s,
    g1_r,
    g2_s,
    g2_r,
    t_s,
    t_r,
    u_s,
    u_r,
):
    b = lax.axis_index("blk")
    w = lax.axis_index("wide")
    slots = nb
    rc = ROW_BLOCKS * EDGE // nb
    gc = RANK // nb
    fr = EDGE // nw
    own = b == w

    def load_x(s):
        return pltpu.make_async_copy(blocks.at[s], x.at[s], x_sem.at[s])

    def start_x(t, carry):
        load_x(lax.rem(b + t, nb)).start()
        return carry

    lax.fori_loop(0, slots, start_x, 0)

    barrier = pltpu.get_barrier_semaphore()

    def signal(i, j):
        pl.semaphore_signal(barrier, inc=1, device_id=(i, j), device_id_type=MESH)

    def greet_blk(d, carry):
        signal(lax.rem(b + d, nb), w)
        return carry

    def greet_wide(d, carry):
        signal(b, lax.rem(w + d, nw))
        return carry

    def greet_cross(v, carry):
        @pl.when(jnp.logical_not(own & (v == w)))
        def _():
            signal(w, v)

        @pl.when(jnp.logical_not(own & (v == b)))
        def _():
            signal(v, b)

        return carry

    lax.fori_loop(1, nb, greet_blk, 0)
    lax.fori_loop(1, nw, greet_wide, 0)
    lax.fori_loop(0, nw, greet_cross, 0)

    @pl.when(own)
    def _():
        pl.semaphore_wait(barrier, nb - 1 + nw - 1 + 2 * (nw - 1))

    @pl.when(jnp.logical_not(own))
    def _():
        pl.semaphore_wait(barrier, nb - 1 + nw - 1 + 2 * nw)

    def send_b(d):
        return pltpu.make_async_remote_copy(
            src_ref=fb,
            dst_ref=bg.at[b],
            send_sem=b_s.at[d],
            recv_sem=b_r.at[b],
            device_id=(lax.rem(b + d, nb), w),
            device_id_type=MESH,
        )

    def recv_b(s):
        return pltpu.make_async_remote_copy(
            src_ref=fb,
            dst_ref=bg.at[s],
            send_sem=b_s.at[0],
            recv_sem=b_r.at[s],
            device_id=(s, w),
            device_id_type=MESH,
        )

    def start_b(d, carry):
        send_b(d).start()
        return carry

    lax.fori_loop(1, nb, start_b, 0)
    bg[b] = fb[...]
    cfull = fc[...].reshape(fc.shape[0] * EDGE, RANK)
    gram_c[...] = lax.dot_general(cfull, cfull, TN, preferred_element_type=F32) * (
        1.0 / cfull.shape[0]
    )
    acc[...] = jnp.zeros_like(acc)
    bd[...] = jnp.zeros_like(bd)

    def share(g, r):
        row = block_row[g].astype(F32)
        return jnp.maximum(0.0, 1.0 - jnp.abs(row - r)) * live[g].astype(F32)

    def first_slot(g):
        crows = fc[block_depth[g]]
        term = jnp.zeros((EDGE, RANK), F32)
        for jg in range(EDGE // 4):
            brows = bg[g, pl.ds(jg * 4 // 16 * 16, 16), :]
            off = jg * 4 % 16
            pair = jnp.concatenate(
                [brows[off + q : off + q + 1, :] * crows for q in range(4)], axis=0
            )
            term += jnp.dot(
                x[g, :, pl.ds(jg * 256, 256)], pair, preferred_element_type=F32
            )
        for r in range(ROW_BLOCKS):
            cut = pl.ds(r * EDGE, EDGE)
            acc[cut, :] = acc[cut, :] + term * share(g, r)

    def first_loop(t, carry):
        g = lax.rem(b + t, nb)
        load_x(g).wait()

        @pl.when(t > 0)
        def _():
            recv_b(g).wait_recv()

        first_slot(g)
        return carry

    lax.fori_loop(0, slots, first_loop, 0)

    def send_ra(d):
        peer = lax.rem(b + d, nb)
        return pltpu.make_async_remote_copy(
            src_ref=acc.at[pl.ds(pl.multiple_of(peer * rc, rc), rc), :],
            dst_ref=ra.at[b],
            send_sem=ra_s.at[d],
            recv_sem=ra_r.at[b],
            device_id=(peer, w),
            device_id_type=MESH,
        )

    def recv_ra(s):
        return pltpu.make_async_remote_copy(
            src_ref=acc.at[pl.ds(0, rc), :],
            dst_ref=ra.at[s],
            send_sem=ra_s.at[0],
            recv_sem=ra_r.at[s],
            device_id=(s, w),
            device_id_type=MESH,
        )

    def start_ra(d, carry):
        send_ra(d).start()
        return carry

    lax.fori_loop(1, nb, start_ra, 0)

    bfull = bg[...].reshape(nb * EDGE, RANK)
    gram_b = lax.dot_general(bfull, bfull, TN, preferred_element_type=F32) * (1.0 / (nb * EDGE))
    eye = lax.broadcasted_iota(jnp.int32, (RANK, RANK), 0) == lax.broadcasted_iota(
        jnp.int32, (RANK, RANK), 1
    )
    mat_a[...] = gram_c[...] * gram_b + jnp.where(eye, RIDGE, 0.0)
    invert_steps(mat_a, 0, RANK // PANEL)

    def sum_ra(d, total):
        s = lax.rem(b + d, nb)
        recv_ra(s).wait_recv()
        return total + ra[s]

    rows_a = lax.fori_loop(1, nb, sum_ra, acc[pl.ds(pl.multiple_of(b * rc, rc), rc), :])
    solved = jnp.dot(
        rows_a, mat_a[...], preferred_element_type=F32, precision=lax.Precision.HIGHEST
    )
    ca[...] = (solved * SCALE).astype(BF16)

    own_rows = pl.ds(pl.multiple_of(b * rc, rc), rc)

    def send_ca(d):
        return pltpu.make_async_remote_copy(
            src_ref=ca,
            dst_ref=fa.at[own_rows, :],
            send_sem=ca_s.at[d],
            recv_sem=ca_r.at[b],
            device_id=(lax.rem(b + d, nb), w),
            device_id_type=MESH,
        )

    def recv_ca(s):
        return pltpu.make_async_remote_copy(
            src_ref=ca,
            dst_ref=fa.at[pl.ds(pl.multiple_of(s * rc, rc), rc), :],
            send_sem=ca_s.at[0],
            recv_sem=ca_r.at[s],
            device_id=(s, w),
            device_id_type=MESH,
        )

    def start_ca(d, carry):
        send_ca(d).start()
        return carry

    def wait_ca(d, carry):
        recv_ca(lax.rem(b + d, nb)).wait_recv()
        return carry

    lax.fori_loop(1, nb, start_ca, 0)
    fa[own_rows, :] = ca[...]
    lax.fori_loop(1, nb, wait_ca, 0)
    out_a[...] = fa[...]

    gl[...] = lax.dot_general(fa[...], fa[...], TN, preferred_element_type=F32)
    own_gram = pl.ds(pl.multiple_of(b * gc, gc), gc)

    def copy_g1(peer, slot, d):
        return pltpu.make_async_remote_copy(
            src_ref=gl.at[own_gram, :],
            dst_ref=gr.at[slot],
            send_sem=g1_s.at[d],
            recv_sem=g1_r.at[slot],
            device_id=(b, peer),
            device_id_type=MESH,
        )

    def start_g1(d, carry):
        copy_g1(lax.rem(w + d, nw), w, d).start()
        return carry

    lax.fori_loop(1, nw, start_g1, 0)

    def copy_t(g, slot):
        return pltpu.make_async_remote_copy(
            src_ref=tsend.at[g],
            dst_ref=trecv.at[slot],
            send_sem=t_s.at[g],
            recv_sem=t_r.at[slot],
            device_id=(b, g),
            device_id_type=MESH,
        )

    def second_slot(g):
        crows = fc[block_depth[g]]
        arows = jnp.zeros((EDGE, RANK), F32)
        for r in range(ROW_BLOCKS):
            arows += fa[pl.ds(r * EDGE, EDGE), :].astype(F32) * share(g, r)
        for q in range(4):
            bd[pl.ds(q * EDGE, EDGE), pl.ds(q * RANK, RANK)] = crows
        lhs = jnp.concatenate(
            [x[g, :, pl.ds(jg * 256, 256)] for jg in range(EDGE // 4)], axis=0
        )
        for q in range(4):
            y[...] = jnp.dot(lhs, bd[:, pl.ds(q * RANK, RANK)], preferred_element_type=F32)
            for jg in range(EDGE // 4):
                prod = y[pl.ds(jg * EDGE, EDGE), :] * arows
                tf[pl.ds(jg * 4 + q, 1), :] = jnp.sum(prod, axis=0, keepdims=True)
        tsend[g] = tf[...].astype(BF16)

    def second_loop(t, carry):
        g = lax.rem(w + 1 + t, nw)
        second_slot(g)

        @pl.when(t < nw - 1)
        def _():
            copy_t(g, w).start()

        return carry

    lax.fori_loop(0, nw // 2, second_loop, 0)

    def sum_g1(d, total):
        s = lax.rem(w + d, nw)
        copy_g1(s, s, 0).wait_recv()
        return total + gr[s]

    gs[...] = lax.fori_loop(1, nw, sum_g1, gl[own_gram, :])

    def copy_g2(peer, rows, slot, d):
        return pltpu.make_async_remote_copy(
            src_ref=gs,
            dst_ref=gfull.at[rows, :],
            send_sem=g2_s.at[d],
            recv_sem=g2_r.at[slot],
            device_id=(peer, w),
            device_id_type=MESH,
        )

    def start_g2(d, carry):
        copy_g2(lax.rem(b + d, nb), own_gram, b, d).start()
        return carry

    lax.fori_loop(1, nb, start_g2, 0)
    gfull[own_gram, :] = gs[...]
    lax.fori_loop(nw // 2, nw, second_loop, 0)

    def wait_g2(d, carry):
        s = lax.rem(b + d, nb)
        copy_g2(s, pl.ds(pl.multiple_of(s * gc, gc), gc), s, 0).wait_recv()
        return carry

    lax.fori_loop(1, nb, wait_g2, 0)
    mat_b[...] = gram_c[...] * (gfull[...] * (1.0 / total_rows)) + jnp.where(eye, RIDGE, 0.0)
    invert_steps(mat_b, 0, RANK // PANEL // 2)

    def sum_t(d, total):
        s = lax.rem(w + d, nw)
        copy_t(s, s).wait_recv()
        return total + trecv[s].astype(F32)

    rows_t = lax.fori_loop(1, nw, sum_t, tf[...])
    for v in range(nw):
        us[v] = rows_t[v * fr : (v + 1) * fr, :]

    def copy_u(v, slot, to_b, to_w):
        return pltpu.make_async_remote_copy(
            src_ref=us.at[v],
            dst_ref=ur.at[slot],
            send_sem=u_s.at[v],
            recv_sem=u_r.at[slot],
            device_id=(to_b, to_w),
            device_id_type=MESH,
        )

    def start_u(v, carry):
        @pl.when(jnp.logical_not(own & (v == w)))
        def _():
            copy_u(v, b, w, v).start()

        return carry

    lax.fori_loop(0, nw, start_u, 0)

    @pl.when(own)
    def _():
        ur[b] = us[w]

    invert_steps(mat_b, RANK // PANEL // 2, RANK // PANEL)

    def sum_u(v, total):
        @pl.when(jnp.logical_not(own & (v == b)))
        def _():
            copy_u(0, v, v, b).wait_recv()

        return total + ur[v]

    rows_b = lax.fori_loop(0, nb, sum_u, jnp.zeros((fr, RANK), F32))
    pad = jnp.concatenate([rows_b] * max(1, 8 // fr), axis=0)
    new_b = jnp.dot(pad, mat_b[...], preferred_element_type=F32, precision=lax.Precision.HIGHEST)
    out_b[...] = (new_b[:fr, :] * SCALE).astype(BF16)

    def drain_blk(d, carry):
        send_b(d).wait_send()
        send_ra(d).wait_send()
        send_ca(d).wait_send()
        copy_g2(lax.rem(b + d, nb), own_gram, b, d).wait_send()
        return carry

    def drain_wide(d, carry):
        peer = lax.rem(w + d, nw)
        copy_g1(peer, w, d).wait_send()
        copy_t(peer, w).wait_send()
        return carry

    def drain_u(v, carry):
        @pl.when(jnp.logical_not(own & (v == w)))
        def _():
            copy_u(v, b, w, v).wait_send()

        return carry

    lax.fori_loop(1, nb, drain_blk, 0)
    lax.fori_loop(1, nw, drain_wide, 0)
    lax.fori_loop(0, nw, drain_u, 0)


def per_device(nb, nw, blocks, block_row, block_depth, live, factor_b, factor_c):
    rows_a = ROW_BLOCKS * EDGE
    rc, gc, fr = rows_a // nb, RANK // nb, EDGE // nw
    vm = pl.BlockSpec(memory_space=pltpu.VMEM)
    sm = pl.BlockSpec(memory_space=pltpu.SMEM)
    dma = pltpu.SemaphoreType.DMA
    return pl.pallas_call(
        functools.partial(kernel, nb, nw, nw * rows_a),
        out_shape=(
            jax.ShapeDtypeStruct((rows_a, RANK), BF16),
            jax.ShapeDtypeStruct((fr, RANK), BF16),
        ),
        in_specs=[sm, sm, sm, pl.BlockSpec(memory_space=pl.ANY), vm, vm],
        out_specs=(vm, vm),
        scratch_shapes=[
            pltpu.VMEM((nb, EDGE, EDGE * EDGE), BF16),
            pltpu.VMEM((nb, EDGE, RANK), BF16),
            pltpu.VMEM((rows_a, RANK), F32),
            pltpu.VMEM((nb, rc, RANK), F32),
            pltpu.VMEM((rc, RANK), BF16),
            pltpu.VMEM((rows_a, RANK), BF16),
            pltpu.VMEM((RANK, RANK), F32),
            pltpu.VMEM((RANK, RANK), F32),
            pltpu.VMEM((RANK, RANK), F32),
            pltpu.VMEM((RANK, RANK), F32),
            pltpu.VMEM((nw, gc, RANK), F32),
            pltpu.VMEM((gc, RANK), F32),
            pltpu.VMEM((RANK, RANK), F32),
            pltpu.VMEM((4 * EDGE, 4 * RANK), BF16),
            pltpu.VMEM((EDGE * EDGE // 4, RANK), F32),
            pltpu.VMEM((EDGE, RANK), F32),
            pltpu.VMEM((nw, EDGE, RANK), BF16),
            pltpu.VMEM((nw, EDGE, RANK), BF16),
            pltpu.VMEM((nw, fr, RANK), F32),
            pltpu.VMEM((nb, fr, RANK), F32),
            dma((nb,)),
            dma((nb,)),
            dma((nb,)),
            dma((nb,)),
            dma((nb,)),
            dma((nb,)),
            dma((nb,)),
            dma((nw,)),
            dma((nw,)),
            dma((nb,)),
            dma((nb,)),
            dma((nw,)),
            dma((nw,)),
            dma((nw,)),
            dma((nb,)),
        ],
        compiler_params=pltpu.CompilerParams(
            collective_id=0, has_side_effects=True, vmem_limit_bytes=60 * 1024 * 1024
        ),
        name="cp_als",
    )(block_row, block_depth, live, blocks, factor_b, factor_c.reshape(-1, EDGE, RANK))


def solution(mesh):
    in_specs = (
        P(("blk", "wide"), None, None),
        P(("blk", "wide")),
        P(("blk", "wide")),
        P(("blk", "wide")),
        P("blk", None),
        P(),
    )
    out_specs = (P("wide", None), P(("blk", "wide"), None))
    body = functools.partial(per_device, mesh.shape["blk"], mesh.shape["wide"])
    return jax.shard_map(
        body, mesh=mesh, in_specs=in_specs, out_specs=out_specs, check_vma=False
    )
```

time: 858 us -> 90.8 us (0.11)
  waiting for transfers between devices: 353 us -> 0 us
  other arithmetic: 146 us -> 0 us
  local copies, waits for them, and re-layouts: 142 us -> 2.83 us
  Pallas kernels: 0 us -> 87.1 us
  loops' own time: 79.6 us -> 0 us
  matrix products: 73.4 us -> 0 us
  blocking collectives: 40.7 us -> 0 us
  between operations: 16.6 us -> 0.64 us
    unnamed x4 -> x0, waiting for transfers between devices: 205 us -> none
    psum x2 -> x0, waiting for transfers between devices: 148 us -> none  [the longest x1 148 us: per_device(): mttkrp_a = lax.psum(mttkrp_part, 'blk')]
    dynamic_slice x128 -> x0, local copies, waits for them, and re-layouts: 113 us -> none  [the longest x32 28 us: second_part(): return second_term(blocks[slot], arows, crows) * weights[slot]]
    another operation x18 -> x0, other arithmetic: 108 us -> none  [the longest x13 68.6 us: factor_solve(): lower = jnp.linalg.cholesky(system)]
    pallas_call x0 -> x1, Pallas kernels: none -> 87.1 us  [per_device(): pl.pallas_call(functools.partial(kernel, nb, nw, nw * rows_a), out_shape=...]
    another operation x4 -> x0, loops' own time: 79.6 us -> none  [the longest x1 55.9 us: per_device(): partials = lax.map(second_part, jnp.arange(slot_total, dtype=jnp.int32))]
    dot_general x35 -> x0, matrix products: 69.3 us -> none  [the longest x16 35.1 us: first_term(): jnp.dot(block, paired.reshape(-1, width), preferred_element_type=jnp.floa...]
    all_gather x1 -> x0, blocking collectives: 40.7 us -> none  [per_device(): piece = lax.all_gather(factor_b, 'blk', axis=0, tiled=True)]
  transfers between devices with their start and end apart: 3 -> 0, of which waited for: 2 -> 0; matrix products, arithmetic and copies ran while one was open for 21% -> 0% of each run, Pallas kernels for 0% -> 0%
where the time goes in v1:
time: 90.8 us; the launch traced here: 90.6 us
  Pallas kernels  87.1 us (96%)
  local copies, waits for them, and re-layouts  2.83 us (3%)
    pallas_call x1, Pallas kernels, per_device(): pl.pallas_call(functools.partial(kernel, nb, nw, nw * rows_a), out_shape=...  87.1 us
    unnamed x2, local copies, waits for them, and re-layouts  2.83 us

profile of v1, /device:TPU:1, one launch (start us, length us, event | category | flops | bytes accessed | tf_op | source)
XLA Modules:
  0.0 90.6 jit_solution(11687765364180796336)
XLA Ops:
  0.6 87.1 %cp_als.1 = (bf16[256,256]{1,0:T(8,128)(2,1)}, bf16[4,256]{1,0:T(4,128)(2,1)}) custom-call(s32[16]{0:T(128)} %block_row.1, s32[16]{0:T(128)} %block_depth.1, s32[16]{0:T(128)} %live.1, bf16[16,64,4096]{2,1,0:T(8,128)(2,1)} %blocks.1, bf16[64,256]{1,0:T(8,128)(2,1)} %fb.1, bf16[16,64,256]{2,1,0:T(8,128)(2,1)} %bitcast.1), custom_call_target="tpu_custom_call" | custom-call | tf_op jit(solution)/shard_map/cp_als/pallas_call | solution.py:528
  87.8 1.6 %copy.10 = bf16[256,256]{1,0:T(8,128)(2,1)} copy(bf16[256,256]{1,0:T(8,128)(2,1)} %get-tuple-element.4) | data formatting | bytes 262144
  89.3 1.3 %copy.11 = bf16[4,256]{1,0:T(4,128)(2,1)} copy(bf16[4,256]{1,0:T(4,128)(2,1)} %get-tuple-element.5) | data formatting | bytes 4096

commit v2 on v1

v2 whole, which is shorter than its diff:
```python
import functools

import jax
import jax.numpy as jnp
from jax import lax
from jax.experimental import pallas as pl
from jax.experimental.pallas import tpu as pltpu
from jax.sharding import PartitionSpec as P

EDGE = 64
RANK = 256
ROW_BLOCKS = 4
RIDGE = 0.05
SCALE = 0.125 / EDGE
PANEL = 32
F32 = jnp.float32
BF16 = jnp.bfloat16
MESH = pl.DeviceIdType.MESH
TN = (((0,), (0,)), ((), ()))


def split3(x):
    hi = x.astype(BF16)
    rest = x - hi.astype(F32)
    mid = rest.astype(BF16)
    low = (rest - mid.astype(F32)).astype(BF16)
    return hi, mid, low


def small_inverse(cols):
    sub = lax.broadcasted_iota(jnp.int32, (8, 128), 0)
    for k in range(8):
        row = [c[k : k + 1, :] for c in cols]
        inv = 1.0 / jnp.broadcast_to(row[k], (8, 128))
        here = sub == k
        pivot_col = cols[k]
        new = []
        for j in range(8):
            if j == k:
                new.append(jnp.where(here, inv, -pivot_col * inv))
            else:
                scaled = row[j] * inv
                new.append(jnp.where(here, scaled, cols[j] - pivot_col * scaled))
        cols = new
    return cols


def panel_eliminate(groups):
    lane = lax.broadcasted_iota(jnp.int32, (8, RANK), 1)
    count = len(groups)
    for s in range(count):
        base = 8 * s
        cols = [
            jnp.broadcast_to(groups[s][:, base + j : base + j + 1], (8, 128)) for j in range(8)
        ]
        others = {
            g: [jnp.broadcast_to(groups[g][:, base + j : base + j + 1], (8, RANK)) for j in range(8)]
            for g in range(count)
            if g != s
        }
        inv = [jnp.concatenate([c, c], axis=1) for c in small_inverse(cols)]
        terms = [inv[j] * groups[s][j : j + 1, :] for j in range(8)]
        while len(terms) > 1:
            terms = [terms[i] + terms[i + 1] for i in range(0, len(terms), 2)]
        rows = terms[0]
        for j in range(8):
            rows = jnp.where(lane == base + j, inv[j], rows)
        inside = (lane >= base) & (lane < base + 8)
        new = []
        for g in range(count):
            if g == s:
                new.append(rows)
                continue
            kept = jnp.where(inside, 0.0, groups[g])
            parts = [others[g][j] * rows[j : j + 1, :] for j in range(8)]
            while len(parts) > 1:
                parts = [parts[i] + parts[i + 1] for i in range(0, len(parts), 2)]
            new.append(kept - parts[0])
        groups = new
    return groups


def invert_steps(mat, first, last):
    lane = lax.broadcasted_iota(jnp.int32, (1, RANK), 1)

    def step(p, carry):
        r0 = pl.multiple_of(p * PANEL, PANEL)
        panel = mat[pl.ds(r0, PANEL), :]
        rolled = pltpu.roll(panel, lax.rem(RANK - r0, RANK), 1)
        groups = panel_eliminate([rolled[8 * g : 8 * g + 8, :] for g in range(PANEL // 8)])
        rows = pltpu.roll(jnp.concatenate(groups, axis=0), r0, 1)
        before = lane < r0
        inside = (lane >= r0) & (lane < r0 + PANEL)
        sign = jnp.where(before, -1.0, jnp.where(inside, 0.0, 1.0))
        qh, qm, ql = split3(panel * sign)
        wh, wm, wl = split3(rows)
        left = jnp.concatenate([qh, qh, qh, qm, qm, ql], axis=0)
        right = jnp.concatenate([wh, wm, wl, wh, wm, wh], axis=0)
        for half in range(2):
            cut = pl.ds(half * 128, 128)
            update = lax.dot_general(
                left[:, half * 128 : half * 128 + 128], right, TN, preferred_element_type=F32
            )
            mat[cut, :] = jnp.where(inside, 0.0, mat[cut, :]) - update
        mat[pl.ds(r0, PANEL), :] = rows
        return carry

    lax.fori_loop(first, last, step, 0)


def kernel(
    nb,
    nw,
    total_rows,
    block_row_in,
    block_depth_in,
    live_in,
    blocks,
    fb_in,
    fc_in,
    out_a,
    out_b,
    block_row,
    block_depth,
    live,
    fb,
    fc,
    x,
    bg,
    acc,
    ra,
    ca,
    fa,
    gram_c,
    mat_a,
    mat_b,
    gl,
    gr,
    gs,
    gfull,
    bd,
    y,
    tf,
    tsend,
    trecv,
    us,
    ur,
    in_sem,
    x_sem,
    bz_s,
    bz_r,
    bx_s,
    bx_r,
    bc_s,
    bc_r,
    ra_s,
    ra_r,
    ca_s,
    ca_r,
    g1_s,
    g1_r,
    g2_s,
    g2_r,
    t_s,
    t_r,
    u_s,
    u_r,
):
    b = lax.axis_index("blk")
    w = lax.axis_index("wide")
    line = nb // 2
    half = EDGE // 2
    rc = ROW_BLOCKS * EDGE // nb
    gc = RANK // nw
    fr = EDGE // nw
    side = b // line
    place = lax.rem(b, line)
    core = lax.rem(w, 2)
    mate = w + 1 - 2 * core
    flip = w + 2 - 4 * lax.rem(w // 2, 2)
    across = (1 - side) * line + place

    def panel(t):
        k = lax.rem(t, line)
        odd = lax.rem(k, 2)
        d = odd * ((k + 1) // 2) + (1 - odd) * lax.rem(line - k // 2, line)
        return lax.rem(side + t // line, 2) * line + lax.rem(place + d, line)

    barrier = pltpu.get_barrier_semaphore()

    def signal(i, j):
        pl.semaphore_signal(barrier, inc=1, device_id=(i, j), device_id_type=MESH)

    def greet_blk(d, carry):
        signal(lax.rem(b + d, nb), w)
        return carry

    def greet_wide(d, carry):
        signal(b, lax.rem(w + d, nw))
        return carry

    lax.fori_loop(1, nb, greet_blk, 0)
    lax.fori_loop(1, nw, greet_wide, 0)
    signal(across, flip)

    small = [
        pltpu.make_async_copy(src, dst, in_sem.at[i])
        for i, (src, dst) in enumerate(
            [
                (fb_in, fb),
                (fc_in, fc),
                (block_row_in, block_row),
                (block_depth_in, block_depth),
                (live_in, live),
            ]
        )
    ]
    for copy in small:
        copy.start()

    def load_x(s):
        return pltpu.make_async_copy(blocks.at[s], x.at[s], x_sem.at[s])

    def start_x(t, carry):
        load_x(panel(t)).start()
        return carry

    lax.fori_loop(0, nb, start_x, 0)
    for copy in small:
        copy.wait()
    bg[b] = fb[...]
    acc[...] = jnp.zeros_like(acc)
    bd[...] = jnp.zeros_like(bd)
    pl.semaphore_wait(barrier, nb - 1 + nw - 1 + 1)

    rows_mine = pl.ds(pl.multiple_of(core * half, half), half)
    rows_mate = pl.ds(pl.multiple_of((1 - core) * half, half), half)

    def copy_bz(to, p):
        return pltpu.make_async_remote_copy(
            src_ref=fb.at[rows_mine, :],
            dst_ref=bg.at[p, rows_mine, :],
            send_sem=bz_s.at[to],
            recv_sem=bz_r.at[p],
            device_id=(to, w),
            device_id_type=MESH,
        )

    def copy_bx(p):
        return pltpu.make_async_remote_copy(
            src_ref=bg.at[p, rows_mine, :],
            dst_ref=bg.at[p, rows_mine, :],
            send_sem=bx_s.at[p],
            recv_sem=bx_r.at[p],
            device_id=(across, flip),
            device_id_type=MESH,
        )

    def copy_bc(p, rows):
        return pltpu.make_async_remote_copy(
            src_ref=bg.at[p, rows, :],
            dst_ref=bg.at[p, rows, :],
            send_sem=bc_s.at[p],
            recv_sem=bc_r.at[p],
            device_id=(b, mate),
            device_id_type=MESH,
        )

    def copy_own_x():
        return pltpu.make_async_remote_copy(
            src_ref=fb.at[rows_mine, :],
            dst_ref=bg.at[b, rows_mine, :],
            send_sem=bx_s.at[b],
            recv_sem=bx_r.at[b],
            device_id=(across, flip),
            device_id_type=MESH,
        )

    def start_bz(t, carry):
        copy_bz(panel(t), b).start()
        return carry

    lax.fori_loop(1, 2, start_bz, 0)
    copy_own_x().start()
    lax.fori_loop(2, line, start_bz, 0)

    def share(g, r):
        row = block_row[g].astype(F32)
        return jnp.maximum(0.0, 1.0 - jnp.abs(row - r)) * live[g].astype(F32)

    def first_slot(g):
        crows = fc[block_depth[g]]
        term = jnp.zeros((EDGE, RANK), F32)
        for jg in range(EDGE // 4):
            brows = bg[g, pl.ds(jg * 4 // 16 * 16, 16), :]
            off = jg * 4 % 16
            pair = jnp.concatenate(
                [brows[off + q : off + q + 1, :] * crows for q in range(4)], axis=0
            )
            term += jnp.dot(
                x[g, :, pl.ds(jg * 256, 256)], pair, preferred_element_type=F32
            )
        for r in range(ROW_BLOCKS):
            cut = pl.ds(r * EDGE, EDGE)
            acc[cut, :] = acc[cut, :] + term * share(g, r)

    def first_loop(t, carry):
        p = panel(t)

        @pl.when((t > 0) & (t < line))
        def _():
            copy_bz(p, p).wait_recv()
            copy_bx(p).start()
            copy_bc(p, rows_mine).start()

        @pl.when((t >= line) & (t < nb))
        def _():
            copy_bx(p).wait_recv()
            copy_bc(p, rows_mine).start()

        @pl.when(t > 1)
        def _():
            copy_bc(panel(t - 1), rows_mate).wait_recv()

        @pl.when(t > 0)
        def _():
            g = panel(t - 1)
            load_x(g).wait()
            first_slot(g)

        return carry

    cfull = fc[...].reshape(fc.shape[0] * EDGE, RANK)
    gram_c[...] = lax.dot_general(cfull, cfull, TN, preferred_element_type=F32) * (
        1.0 / cfull.shape[0]
    )
    lax.fori_loop(0, nb + 1, first_loop, 0)

    def copy_ra(peer, slot):
        return pltpu.make_async_remote_copy(
            src_ref=acc.at[pl.ds(pl.multiple_of(peer * rc, rc), rc), :],
            dst_ref=ra.at[slot],
            send_sem=ra_s.at[peer],
            recv_sem=ra_r.at[slot],
            device_id=(peer, w),
            device_id_type=MESH,
        )

    def start_ra(t, carry):
        copy_ra(panel(nb - t), b).start()
        return carry

    lax.fori_loop(1, nb, start_ra, 0)

    bfull = bg[...].reshape(nb * EDGE, RANK)
    gram_b = lax.dot_general(bfull, bfull, TN, preferred_element_type=F32) * (1.0 / (nb * EDGE))
    eye = lax.broadcasted_iota(jnp.int32, (RANK, RANK), 0) == lax.broadcasted_iota(
        jnp.int32, (RANK, RANK), 1
    )
    mat_a[...] = gram_c[...] * gram_b + jnp.where(eye, RIDGE, 0.0)
    invert_steps(mat_a, 0, RANK // PANEL)

    own_rows = pl.ds(pl.multiple_of(b * rc, rc), rc)

    def sum_ra(t, total):
        s = panel(t)
        copy_ra(s, s).wait_recv()
        return total + ra[s]

    rows_a = lax.fori_loop(1, nb, sum_ra, acc[own_rows, :])
    solved = jnp.dot(
        rows_a, mat_a[...], preferred_element_type=F32, precision=lax.Precision.HIGHEST
    )
    ca[...] = (solved * SCALE).astype(BF16)

    def copy_ca(peer, s):
        return pltpu.make_async_remote_copy(
            src_ref=ca,
            dst_ref=fa.at[pl.ds(pl.multiple_of(s * rc, rc), rc), :],
            send_sem=ca_s.at[peer],
            recv_sem=ca_r.at[s],
            device_id=(peer, w),
            device_id_type=MESH,
        )

    def start_ca(t, carry):
        copy_ca(panel(nb - t), b).start()
        return carry

    def wait_ca(t, carry):
        s = panel(t)
        copy_ca(s, s).wait_recv()
        return carry

    lax.fori_loop(1, nb, start_ca, 0)
    fa[own_rows, :] = ca[...]
    lax.fori_loop(1, nb, wait_ca, 0)

    gl[...] = lax.dot_general(fa[...], fa[...], TN, preferred_element_type=F32)

    def gram_rows(v):
        return pl.ds(pl.multiple_of(v * gc, gc), gc)

    def copy_g1(peer, slot):
        return pltpu.make_async_remote_copy(
            src_ref=gl.at[gram_rows(peer), :],
            dst_ref=gr.at[slot],
            send_sem=g1_s.at[peer],
            recv_sem=g1_r.at[slot],
            device_id=(b, peer),
            device_id_type=MESH,
        )

    def start_g1(d, carry):
        copy_g1(lax.rem(w + d, nw), w).start()
        return carry

    lax.fori_loop(1, nw, start_g1, 0)
    out_a[...] = fa[...]

    def copy_t(peer, slot):
        return pltpu.make_async_remote_copy(
            src_ref=tsend.at[peer],
            dst_ref=trecv.at[slot],
            send_sem=t_s.at[peer],
            recv_sem=t_r.at[slot],
            device_id=(peer, w),
            device_id_type=MESH,
        )

    def second_slot(g):
        crows = fc[block_depth[g]]
        arows = jnp.zeros((EDGE, RANK), F32)
        for r in range(ROW_BLOCKS):
            arows += fa[pl.ds(r * EDGE, EDGE), :].astype(F32) * share(g, r)
        for q in range(4):
            bd[pl.ds(q * EDGE, EDGE), pl.ds(q * RANK, RANK)] = crows
        lhs = jnp.concatenate(
            [x[g, :, pl.ds(jg * 256, 256)] for jg in range(EDGE // 4)], axis=0
        )
        for q in range(4):
            y[...] = jnp.dot(lhs, bd[:, pl.ds(q * RANK, RANK)], preferred_element_type=F32)
            for jg in range(EDGE // 4):
                prod = y[pl.ds(jg * EDGE, EDGE), :] * arows
                tf[pl.ds(jg * 4 + q, 1), :] = jnp.sum(prod, axis=0, keepdims=True)
        tsend[g] = tf[...].astype(BF16)

    def copy_g2(peer, s):
        return pltpu.make_async_remote_copy(
            src_ref=gs,
            dst_ref=gfull.at[gram_rows(s), :],
            send_sem=g2_s.at[peer],
            recv_sem=g2_r.at[s],
            device_id=(b, peer),
            device_id_type=MESH,
        )

    def second_loop(t, carry):
        g = panel(nb - 1 - t)

        @pl.when(t == nb * 3 // 8)
        def _():
            def sum_g1(d, total):
                s = lax.rem(w + d, nw)
                copy_g1(s, s).wait_recv()
                return total + gr[s]

            def start_g2(d, carry):
                copy_g2(lax.rem(w + d, nw), w).start()
                return carry

            gs[...] = lax.fori_loop(1, nw, sum_g1, gl[gram_rows(w), :])
            lax.fori_loop(1, nw, start_g2, 0)

        second_slot(g)

        @pl.when(t < nb - 1)
        def _():
            copy_t(g, b).start()

        return carry

    lax.fori_loop(0, nb, second_loop, 0)
    gfull[gram_rows(w), :] = gs[...]

    def wait_g2(d, carry):
        s = lax.rem(w + d, nw)
        copy_g2(s, s).wait_recv()
        return carry

    lax.fori_loop(1, nw, wait_g2, 0)
    mat_b[...] = gram_c[...] * (gfull[...] * (1.0 / total_rows)) + jnp.where(eye, RIDGE, 0.0)
    invert_steps(mat_b, 0, RANK // PANEL // 2)

    def sum_t(t, total):
        s = panel(nb - t)
        copy_t(s, s).wait_recv()
        return total + trecv[s].astype(F32)

    rows_t = lax.fori_loop(1, nb, sum_t, tf[...])
    for v in range(nw):
        us[v] = rows_t[v * fr : (v + 1) * fr, :]

    def copy_u(peer, slot):
        return pltpu.make_async_remote_copy(
            src_ref=us.at[peer],
            dst_ref=ur.at[slot],
            send_sem=u_s.at[peer],
            recv_sem=u_r.at[slot],
            device_id=(b, peer),
            device_id_type=MESH,
        )

    def start_u(d, carry):
        copy_u(lax.rem(w + d, nw), w).start()
        return carry

    lax.fori_loop(1, nw, start_u, 0)
    invert_steps(mat_b, RANK // PANEL // 2, RANK // PANEL)

    def sum_u(d, total):
        s = lax.rem(w + d, nw)
        copy_u(s, s).wait_recv()
        return total + ur[s]

    rows_b = lax.fori_loop(1, nw, sum_u, us[w])
    pad = jnp.concatenate([rows_b] * max(1, 8 // fr), axis=0)
    new_b = jnp.dot(pad, mat_b[...], preferred_element_type=F32, precision=lax.Precision.HIGHEST)
    out_b[...] = (new_b[:fr, :] * SCALE).astype(BF16)

    def drain_line(t, carry):
        p = panel(t)
        copy_bz(p, b).wait_send()
        copy_bx(p).wait_send()
        return carry

    def drain_blk(t, carry):
        p = panel(t)
        copy_bc(p, rows_mine).wait_send()
        copy_ra(p, b).wait_send()
        copy_ca(p, b).wait_send()
        copy_t(p, b).wait_send()
        return carry

    def drain_wide(d, carry):
        peer = lax.rem(w + d, nw)
        copy_g1(peer, w).wait_send()
        copy_g2(peer, w).wait_send()
        copy_u(peer, w).wait_send()
        return carry

    copy_own_x().wait_send()
    lax.fori_loop(1, line, drain_line, 0)
    lax.fori_loop(1, nb, drain_blk, 0)
    lax.fori_loop(1, nw, drain_wide, 0)


def per_device(nb, nw, blocks, block_row, block_depth, live, factor_b, factor_c):
    rows_a = ROW_BLOCKS * EDGE
    rc, gc, fr = rows_a // nb, RANK // nw, EDGE // nw
    vm = pl.BlockSpec(memory_space=pltpu.VMEM)
    depth = factor_c.shape[0] // EDGE
    dma = pltpu.SemaphoreType.DMA
    return pl.pallas_call(
        functools.partial(kernel, nb, nw, nw * rows_a),
        out_shape=(
            jax.ShapeDtypeStruct((rows_a, RANK), BF16),
            jax.ShapeDtypeStruct((fr, RANK), BF16),
        ),
        in_specs=[pl.BlockSpec(memory_space=pl.ANY)] * 6,
        out_specs=(vm, vm),
        scratch_shapes=[
            pltpu.SMEM((nb,), jnp.int32),
            pltpu.SMEM((nb,), jnp.int32),
            pltpu.SMEM((nb,), jnp.int32),
            pltpu.VMEM((EDGE, RANK), BF16),
            pltpu.VMEM((depth, EDGE, RANK), BF16),
            pltpu.VMEM((nb, EDGE, EDGE * EDGE), BF16),
            pltpu.VMEM((nb, EDGE, RANK), BF16),
            pltpu.VMEM((rows_a, RANK), F32),
            pltpu.VMEM((nb, rc, RANK), F32),
            pltpu.VMEM((rc, RANK), BF16),
            pltpu.VMEM((rows_a, RANK), BF16),
            pltpu.VMEM((RANK, RANK), F32),
            pltpu.VMEM((RANK, RANK), F32),
            pltpu.VMEM((RANK, RANK), F32),
            pltpu.VMEM((RANK, RANK), F32),
            pltpu.VMEM((nw, gc, RANK), F32),
            pltpu.VMEM((gc, RANK), F32),
            pltpu.VMEM((RANK, RANK), F32),
            pltpu.VMEM((4 * EDGE, 4 * RANK), BF16),
            pltpu.VMEM((EDGE * EDGE // 4, RANK), F32),
            pltpu.VMEM((EDGE, RANK), F32),
            pltpu.VMEM((nb, EDGE, RANK), BF16),
            pltpu.VMEM((nb, EDGE, RANK), BF16),
            pltpu.VMEM((nw, fr, RANK), F32),
            pltpu.VMEM((nw, fr, RANK), F32),
            dma((5,)),
            dma((nb,)),
            dma((nb,)),
            dma((nb,)),
            dma((nb,)),
            dma((nb,)),
            dma((nb,)),
            dma((nb,)),
            dma((nb,)),
            dma((nb,)),
            dma((nb,)),
            dma((nb,)),
            dma((nw,)),
            dma((nw,)),
            dma((nw,)),
            dma((nw,)),
            dma((nb,)),
            dma((nb,)),
            dma((nw,)),
            dma((nw,)),
        ],
        compiler_params=pltpu.CompilerParams(
            collective_id=0, has_side_effects=True, vmem_limit_bytes=60 * 1024 * 1024
        ),
        name="cp_als",
    )(block_row, block_depth, live, blocks, factor_b, factor_c.reshape(-1, EDGE, RANK))


def solution(mesh):
    in_specs = (
        P(("blk", "wide"), None, None),
        P(("blk", "wide")),
        P(("blk", "wide")),
        P(("blk", "wide")),
        P("blk", None),
        P(),
    )
    out_specs = (P("wide", None), P(("blk", "wide"), None))
    body = functools.partial(per_device, mesh.shape["blk"], mesh.shape["wide"])
    return jax.shard_map(
        body, mesh=mesh, in_specs=in_specs, out_specs=out_specs, check_vma=False
    )
```

time: 90.8 us -> 79.7 us (0.88)
  Pallas kernels: 87.1 us -> 76.1 us
    pallas_call x1, Pallas kernels: 87.1 us -> 76.1 us  [per_device(): pl.pallas_call(functools.partial(kernel, nb, nw, nw * rows_a), out_shape=...]
where the time goes in v2:
time: 79.7 us; the launch traced here: 79.6 us
  Pallas kernels  76.1 us (95%)
  local copies, waits for them, and re-layouts  2.83 us (4%)
    pallas_call x1, Pallas kernels, per_device(): pl.pallas_call(functools.partial(kernel, nb, nw, nw * rows_a), out_shape=...  76.1 us
    unnamed x2, local copies, waits for them, and re-layouts  2.83 us

profile of v2, /device:TPU:1, one launch (start us, length us, event | category | flops | bytes accessed | tf_op | source)
XLA Modules:
  0.0 79.6 jit_solution(9147205235129730170)
XLA Ops:
  0.6 76.1 %cp_als.1 = (bf16[256,256]{1,0:T(8,128)(2,1)}, bf16[4,256]{1,0:T(4,128)(2,1)}) custom-call(s32[16]{0:T(128)} %block_row_in.1, s32[16]{0:T(128)} %block_depth_in.1, s32[16]{0:T(128)} %live_in.1, bf16[16,64,4096]{2,1,0:T(8,128)(2,1)} %blocks.1, bf16[64,256]{1,0:T(8,128)(2,1)} %fb_in.1, bf16[16,64,256]{2,1,0:T(8,128)(2,1)} %bitcast.1), custom_call_target="tpu_custom_call" | custom-call | tf_op jit(solution)/shard_map/cp_als/pallas_call | solution.py:564
  76.7 1.6 %copy.10 = bf16[256,256]{1,0:T(8,128)(2,1)} copy(bf16[256,256]{1,0:T(8,128)(2,1)} %get-tuple-element.4) | data formatting | bytes 262144
  78.3 1.3 %copy.11 = bf16[4,256]{1,0:T(4,128)(2,1)} copy(bf16[4,256]{1,0:T(4,128)(2,1)} %get-tuple-element.5) | data formatting | bytes 4096

commit v3 on v2

--- a/solution.py
+++ b/solution.py
@@ -12,7 +12,9 @@
 ROW_BLOCKS = 4
 RIDGE = 0.05
 SCALE = 0.125 / EDGE
-PANEL = 32
+PANEL = 64
+LAG = 3
+EARLY = 7
 F32 = jnp.float32
 BF16 = jnp.bfloat16
 MESH = pl.DeviceIdType.MESH
@@ -29,18 +31,24 @@
 
 def small_inverse(cols):
     sub = lax.broadcasted_iota(jnp.int32, (8, 128), 0)
-    for k in range(8):
-        row = [c[k : k + 1, :] for c in cols]
-        inv = 1.0 / jnp.broadcast_to(row[k], (8, 128))
-        here = sub == k
-        pivot_col = cols[k]
+    for k in range(0, 8, 2):
+        row0 = [jnp.broadcast_to(c[k : k + 1, :], (8, 128)) for c in cols]
+        row1 = [jnp.broadcast_to(c[k + 1 : k + 2, :], (8, 128)) for c in cols]
+        p, q, r, s = row0[k], row0[k + 1], row1[k], row1[k + 1]
+        inv = 1.0 / (p * s - q * r)
+        col0, col1 = cols[k], cols[k + 1]
         new = []
         for j in range(8):
             if j == k:
-                new.append(jnp.where(here, inv, -pivot_col * inv))
+                up, low = s * inv, -(r * inv)
+            elif j == k + 1:
+                up, low = -(q * inv), p * inv
             else:
-                scaled = row[j] * inv
-                new.append(jnp.where(here, scaled, cols[j] - pivot_col * scaled))
+                up = (s * row0[j] - q * row1[j]) * inv
+                low = (p * row1[j] - r * row0[j]) * inv
+            drop = col0 * up + col1 * low
+            rest = -drop if j in (k, k + 1) else cols[j] - drop
+            new.append(jnp.where(sub == k, up, jnp.where(sub == k + 1, low, rest)))
         cols = new
     return cols
 
@@ -140,11 +148,15 @@
     gfull,
     bd,
     y,
+    yc,
     tf,
     tsend,
     trecv,
     us,
     ur,
+    cs,
+    cr,
+    tm,
     in_sem,
     x_sem,
     bz_s,
@@ -165,11 +177,14 @@
     t_r,
     u_s,
     u_r,
+    p_s,
+    p_r,
 ):
     b = lax.axis_index("blk")
     w = lax.axis_index("wide")
     line = nb // 2
     half = EDGE // 2
+    early = EARLY * nb // 16
     rc = ROW_BLOCKS * EDGE // nb
     gc = RANK // nw
     fr = EDGE // nw
@@ -185,6 +200,15 @@
         odd = lax.rem(k, 2)
         d = odd * ((k + 1) // 2) + (1 - odd) * lax.rem(line - k // 2, line)
         return lax.rem(side + t // line, 2) * line + lax.rem(place + d, line)
+
+    def slot_of(t):
+        pairs = line // 2
+        u = t // 2
+        k = lax.rem(u, pairs)
+        pair = lax.rem(place // 2 + pairs - 1 - k, pairs)
+        far = 1 - u // pairs
+        which = lax.rem(t, 2) * core + (1 - lax.rem(t, 2)) * (1 - core)
+        return lax.rem(side + far, 2) * line + pair * 2 + which
 
     barrier = pltpu.get_barrier_semaphore()
 
@@ -318,13 +342,13 @@
             copy_bx(p).wait_recv()
             copy_bc(p, rows_mine).start()
 
-        @pl.when(t > 1)
-        def _():
-            copy_bc(panel(t - 1), rows_mate).wait_recv()
-
-        @pl.when(t > 0)
-        def _():
-            g = panel(t - 1)
+        @pl.when(t > LAG)
+        def _():
+            copy_bc(panel(t - LAG), rows_mate).wait_recv()
+
+        @pl.when(t >= LAG)
+        def _():
+            g = panel(t - LAG)
             load_x(g).wait()
             first_slot(g)
 
@@ -334,7 +358,7 @@
     gram_c[...] = lax.dot_general(cfull, cfull, TN, preferred_element_type=F32) * (
         1.0 / cfull.shape[0]
     )
-    lax.fori_loop(0, nb + 1, first_loop, 0)
+    lax.fori_loop(1, nb + LAG, first_loop, 0)
 
     def copy_ra(peer, slot):
         return pltpu.make_async_remote_copy(
@@ -394,6 +418,24 @@
 
     lax.fori_loop(1, nb, start_ca, 0)
     fa[own_rows, :] = ca[...]
+
+    def depth_operands(g):
+        crows = fc[block_depth[g]]
+        for q in range(4):
+            bd[pl.ds(q * EDGE, EDGE), pl.ds(q * RANK, RANK)] = crows
+        return jnp.concatenate(
+            [x[g, :, pl.ds(jg * 256, 256)] for jg in range(EDGE // 4)], axis=0
+        )
+
+    def early_loop(t, carry):
+        lhs = depth_operands(slot_of(t))
+        for q in range(4):
+            yc[t, q] = jnp.dot(
+                lhs, bd[:, pl.ds(q * RANK, RANK)], preferred_element_type=F32
+            ).astype(BF16)
+        return carry
+
+    lax.fori_loop(0, early, early_loop, 0)
     lax.fori_loop(1, nb, wait_ca, 0)
 
     gl[...] = lax.dot_general(fa[...], fa[...], TN, preferred_element_type=F32)
@@ -428,22 +470,27 @@
             device_id_type=MESH,
         )
 
-    def second_slot(g):
-        crows = fc[block_depth[g]]
+    def weighted_rows(g):
         arows = jnp.zeros((EDGE, RANK), F32)
         for r in range(ROW_BLOCKS):
             arows += fa[pl.ds(r * EDGE, EDGE), :].astype(F32) * share(g, r)
-        for q in range(4):
-            bd[pl.ds(q * EDGE, EDGE), pl.ds(q * RANK, RANK)] = crows
-        lhs = jnp.concatenate(
-            [x[g, :, pl.ds(jg * 256, 256)] for jg in range(EDGE // 4)], axis=0
-        )
+        return arows
+
+    def second_slot(g):
+        arows = weighted_rows(g)
+        lhs = depth_operands(g)
         for q in range(4):
             y[...] = jnp.dot(lhs, bd[:, pl.ds(q * RANK, RANK)], preferred_element_type=F32)
             for jg in range(EDGE // 4):
                 prod = y[pl.ds(jg * EDGE, EDGE), :] * arows
                 tf[pl.ds(jg * 4 + q, 1), :] = jnp.sum(prod, axis=0, keepdims=True)
-        tsend[g] = tf[...].astype(BF16)
+
+    def second_early(t, g):
+        arows = weighted_rows(g)
+        for q in range(4):
+            for jg in range(EDGE // 4):
+                prod = yc[t, q, pl.ds(jg * EDGE, EDGE), :].astype(F32) * arows
+                tf[pl.ds(jg * 4 + q, 1), :] = jnp.sum(prod, axis=0, keepdims=True)
 
     def copy_g2(peer, s):
         return pltpu.make_async_remote_copy(
@@ -455,10 +502,48 @@
             device_id_type=MESH,
         )
 
+    def copy_pair(u):
+        return pltpu.make_async_remote_copy(
+            src_ref=cs.at[u],
+            dst_ref=cr.at[u],
+            send_sem=p_s.at[u],
+            recv_sem=p_r.at[u],
+            device_id=(b, mate),
+            device_id_type=MESH,
+        )
+
+    def pass_on(u):
+        copy_pair(u).wait_recv()
+        g = slot_of(2 * u + 1)
+        tsend[g] = (tm[u] + cr[u]).astype(BF16)
+
+        @pl.when(g != b)
+        def _():
+            copy_t(g, b).start()
+
+    def after_slot(t):
+        u = t // 2
+
+        @pl.when(lax.rem(t, 2) == 0)
+        def _():
+            cs[u] = tf[...]
+            copy_pair(u).start()
+
+        @pl.when(lax.rem(t, 2) == 1)
+        def _():
+            tm[u] = tf[...]
+
+            @pl.when(u > 0)
+            def _():
+                pass_on(u - 1)
+
+    def second_first(t, carry):
+        second_early(t, slot_of(t))
+        after_slot(t)
+        return carry
+
     def second_loop(t, carry):
-        g = panel(nb - 1 - t)
-
-        @pl.when(t == nb * 3 // 8)
+        @pl.when(t == nb // 2)
         def _():
             def sum_g1(d, total):
                 s = lax.rem(w + d, nw)
@@ -472,15 +557,13 @@
             gs[...] = lax.fori_loop(1, nw, sum_g1, gl[gram_rows(w), :])
             lax.fori_loop(1, nw, start_g2, 0)
 
-        second_slot(g)
-
-        @pl.when(t < nb - 1)
-        def _():
-            copy_t(g, b).start()
-
-        return carry
-
-    lax.fori_loop(0, nb, second_loop, 0)
+        second_slot(slot_of(t))
+        after_slot(t)
+        return carry
+
+    lax.fori_loop(0, early, second_first, 0)
+    lax.fori_loop(early, nb, second_loop, 0)
+    pass_on(nb // 2 - 1)
     gfull[gram_rows(w), :] = gs[...]
 
     def wait_g2(d, carry):
@@ -492,14 +575,19 @@
     mat_b[...] = gram_c[...] * (gfull[...] * (1.0 / total_rows)) + jnp.where(eye, RIDGE, 0.0)
     invert_steps(mat_b, 0, RANK // PANEL // 2)
 
-    def sum_t(t, total):
-        s = panel(nb - t)
-        copy_t(s, s).wait_recv()
-        return total + trecv[s].astype(F32)
-
-    rows_t = lax.fori_loop(1, nb, sum_t, tf[...])
-    for v in range(nw):
-        us[v] = rows_t[v * fr : (v + 1) * fr, :]
+    holds = lax.rem(b, 2) == core
+
+    @pl.when(holds)
+    def _():
+        def sum_t(t, total):
+            s = panel(nb - t)
+            copy_t(s, s).wait_recv()
+            return total + trecv[s].astype(F32)
+
+        own_t = tm[nb // 2 - 1] + cr[nb // 2 - 1]
+        rows_t = lax.fori_loop(1, nb, sum_t, own_t)
+        for v in range(nw):
+            us[v] = rows_t[v * fr : (v + 1) * fr, :]
 
     def copy_u(peer, slot):
         return pltpu.make_async_remote_copy(
@@ -515,15 +603,26 @@
         copy_u(lax.rem(w + d, nw), w).start()
         return carry
 
-    lax.fori_loop(1, nw, start_u, 0)
+    @pl.when(holds)
+    def _():
+        lax.fori_loop(1, nw, start_u, 0)
+
     invert_steps(mat_b, RANK // PANEL // 2, RANK // PANEL)
 
-    def sum_u(d, total):
-        s = lax.rem(w + d, nw)
-        copy_u(s, s).wait_recv()
+    @pl.when(holds)
+    def _():
+        ur[w] = us[w]
+
+    def sum_u(i, total):
+        s = 2 * i + lax.rem(b, 2)
+
+        @pl.when(s != w)
+        def _():
+            copy_u(s, s).wait_recv()
+
         return total + ur[s]
 
-    rows_b = lax.fori_loop(1, nw, sum_u, us[w])
+    rows_b = lax.fori_loop(0, nw // 2, sum_u, jnp.zeros((fr, RANK), F32))
     pad = jnp.concatenate([rows_b] * max(1, 8 // fr), axis=0)
     new_b = jnp.dot(pad, mat_b[...], preferred_element_type=F32, precision=lax.Precision.HIGHEST)
     out_b[...] = (new_b[:fr, :] * SCALE).astype(BF16)
@@ -539,20 +638,33 @@
         copy_bc(p, rows_mine).wait_send()
         copy_ra(p, b).wait_send()
         copy_ca(p, b).wait_send()
-        copy_t(p, b).wait_send()
+
+        @pl.when(lax.rem(p, 2) == core)
+        def _():
+            copy_t(p, b).wait_send()
+
         return carry
 
     def drain_wide(d, carry):
         peer = lax.rem(w + d, nw)
         copy_g1(peer, w).wait_send()
         copy_g2(peer, w).wait_send()
-        copy_u(peer, w).wait_send()
+
+        @pl.when(holds)
+        def _():
+            copy_u(peer, w).wait_send()
+
+        return carry
+
+    def drain_pair(u, carry):
+        copy_pair(u).wait_send()
         return carry
 
     copy_own_x().wait_send()
     lax.fori_loop(1, line, drain_line, 0)
     lax.fori_loop(1, nb, drain_blk, 0)
     lax.fori_loop(1, nw, drain_wide, 0)
+    lax.fori_loop(0, nb // 2, drain_pair, 0)
 
 
 def per_device(nb, nw, blocks, block_row, block_depth, live, factor_b, factor_c):
@@ -567,7 +679,7 @@
             jax.ShapeDtypeStruct((rows_a, RANK), BF16),
             jax.ShapeDtypeStruct((fr, RANK), BF16),
         ),
-        in_specs=[pl.BlockSpec(memory_space=pl.ANY)] * 6,
+        in_specs=[pl.BlockSpec(memory_space=pltpu.HBM)] * 6,
         out_specs=(vm, vm),
         scratch_shapes=[
             pltpu.SMEM((nb,), jnp.int32),
@@ -590,11 +702,15 @@
             pltpu.VMEM((RANK, RANK), F32),
             pltpu.VMEM((4 * EDGE, 4 * RANK), BF16),
             pltpu.VMEM((EDGE * EDGE // 4, RANK), F32),
+            pltpu.VMEM((EARLY * nb // 16, 4, EDGE * EDGE // 4, RANK), BF16),
             pltpu.VMEM((EDGE, RANK), F32),
             pltpu.VMEM((nb, EDGE, RANK), BF16),
             pltpu.VMEM((nb, EDGE, RANK), BF16),
             pltpu.VMEM((nw, fr, RANK), F32),
             pltpu.VMEM((nw, fr, RANK), F32),
+            pltpu.VMEM((nb // 2, EDGE, RANK), F32),
+            pltpu.VMEM((nb // 2, EDGE, RANK), F32),
+            pltpu.VMEM((nb // 2, EDGE, RANK), F32),
             dma((5,)),
             dma((nb,)),
             dma((nb,)),
@@ -615,9 +731,11 @@
             dma((nb,)),
             dma((nw,)),
             dma((nw,)),
+            dma((nb // 2,)),
+            dma((nb // 2,)),
         ],
         compiler_params=pltpu.CompilerParams(
-            collective_id=0, has_side_effects=True, vmem_limit_bytes=60 * 1024 * 1024
+            collective_id=0, has_side_effects=True, vmem_limit_bytes=54 * 1024 * 1024
         ),
         name="cp_als",
     )(block_row, block_depth, live, blocks, factor_b, factor_c.reshape(-1, EDGE, RANK))

time: 79.7 us -> 72.4 us (0.908)
  Pallas kernels: 76.1 us -> 68.8 us
    pallas_call x1, Pallas kernels: 76.1 us -> 68.8 us  [per_device(): pl.pallas_call(functools.partial(kernel, nb, nw, nw * rows_a), out_shape=...]
where the time goes in v3:
time: 72.4 us; the launch traced here: 72.2 us
  Pallas kernels  68.8 us (95%)
  local copies, waits for them, and re-layouts  2.83 us (4%)
    pallas_call x1, Pallas kernels, per_device(): pl.pallas_call(functools.partial(kernel, nb, nw, nw * rows_a), out_shape=...  68.8 us
    unnamed x2, local copies, waits for them, and re-layouts  2.83 us

profile of v3, /device:TPU:1, one launch (start us, length us, event | category | flops | bytes accessed | tf_op | source)
XLA Modules:
  0.0 72.2 jit_solution(43271170148421242)
XLA Ops:
  0.6 68.8 %cp_als.1 = (bf16[256,256]{1,0:T(8,128)(2,1)}, bf16[4,256]{1,0:T(4,128)(2,1)}) custom-call(s32[16]{0:T(128)} %block_row_in.1, s32[16]{0:T(128)} %block_depth_in.1, s32[16]{0:T(128)} %live_in.1, bf16[16,64,4096]{2,1,0:T(8,128)(2,1)} %blocks.1, bf16[64,256]{1,0:T(8,128)(2,1)} %fb_in.1, bf16[16,64,256]{2,1,0:T(8,128)(2,1)} %bitcast.1), custom_call_target="tpu_custom_call" | custom-call | tf_op jit(solution)/shard_map/cp_als/pallas_call | solution.py:676
  69.4 1.6 %copy.10 = bf16[256,256]{1,0:T(8,128)(2,1)} copy(bf16[256,256]{1,0:T(8,128)(2,1)} %get-tuple-element.4) | data formatting | bytes 262144
  71.0 1.3 %copy.11 = bf16[4,256]{1,0:T(4,128)(2,1)} copy(bf16[4,256]{1,0:T(4,128)(2,1)} %get-tuple-element.5) | data formatting | bytes 4096

commit v4 on v3

--- a/solution.py
+++ b/solution.py
@@ -53,8 +53,15 @@
     return cols
 
 
+def tree_sum(terms):
+    while len(terms) > 1:
+        terms = [terms[i] + terms[i + 1] for i in range(0, len(terms), 2)]
+    return terms[0]
+
+
 def panel_eliminate(groups):
     lane = lax.broadcasted_iota(jnp.int32, (8, RANK), 1)
+    bits = [(lane & (1 << i)) != 0 for i in range(3)]
     count = len(groups)
     for s in range(count):
         base = 8 * s
@@ -67,24 +74,23 @@
             if g != s
         }
         inv = [jnp.concatenate([c, c], axis=1) for c in small_inverse(cols)]
-        terms = [inv[j] * groups[s][j : j + 1, :] for j in range(8)]
-        while len(terms) > 1:
-            terms = [terms[i] + terms[i + 1] for i in range(0, len(terms), 2)]
-        rows = terms[0]
-        for j in range(8):
-            rows = jnp.where(lane == base + j, inv[j], rows)
+        placed = inv
+        for bit in bits:
+            placed = [
+                jnp.where(bit, placed[i + 1], placed[i]) for i in range(0, len(placed), 2)
+            ]
         inside = (lane >= base) & (lane < base + 8)
-        new = []
-        for g in range(count):
-            if g == s:
-                new.append(rows)
-                continue
-            kept = jnp.where(inside, 0.0, groups[g])
-            parts = [others[g][j] * rows[j : j + 1, :] for j in range(8)]
-            while len(parts) > 1:
-                parts = [parts[i] + parts[i + 1] for i in range(0, len(parts), 2)]
-            new.append(kept - parts[0])
-        groups = new
+        rows = jnp.where(
+            inside, placed[0], tree_sum([inv[j] * groups[s][j : j + 1, :] for j in range(8)])
+        )
+        spread = [jnp.broadcast_to(rows[j : j + 1, :], (8, RANK)) for j in range(8)]
+        groups = [
+            rows
+            if g == s
+            else jnp.where(inside, 0.0, groups[g])
+            - tree_sum([others[g][j] * spread[j] for j in range(8)])
+            for g in range(count)
+        ]
     return groups
 
 

time: 72.4 us -> 71.5 us (0.988)
  Pallas kernels: 68.8 us -> 67.9 us
    pallas_call x1, Pallas kernels: 68.8 us -> 67.9 us  [per_device(): pl.pallas_call(functools.partial(kernel, nb, nw, nw * rows_a), out_shape=...]
where the time goes in v4:
time: 71.5 us; the launch traced here: 71.4 us
  Pallas kernels  67.9 us (95%)
  local copies, waits for them, and re-layouts  2.83 us (4%)
    pallas_call x1, Pallas kernels, per_device(): pl.pallas_call(functools.partial(kernel, nb, nw, nw * rows_a), out_shape=...  67.9 us
    unnamed x2, local copies, waits for them, and re-layouts  2.83 us

profile of v4, /device:TPU:1, one launch (start us, length us, event | category | flops | bytes accessed | tf_op | source)
XLA Modules:
  0.0 71.4 jit_solution(5044895260927834969)
XLA Ops:
  0.6 67.9 %cp_als.1 = (bf16[256,256]{1,0:T(8,128)(2,1)}, bf16[4,256]{1,0:T(4,128)(2,1)}) custom-call(s32[16]{0:T(128)} %block_row_in.1, s32[16]{0:T(128)} %block_depth_in.1, s32[16]{0:T(128)} %live_in.1, bf16[16,64,4096]{2,1,0:T(8,128)(2,1)} %blocks.1, bf16[64,256]{1,0:T(8,128)(2,1)} %fb_in.1, bf16[16,64,256]{2,1,0:T(8,128)(2,1)} %bitcast.1), custom_call_target="tpu_custom_call" | custom-call | tf_op jit(solution)/shard_map/cp_als/pallas_call | solution.py:682
  68.6 1.6 %copy.10 = bf16[256,256]{1,0:T(8,128)(2,1)} copy(bf16[256,256]{1,0:T(8,128)(2,1)} %get-tuple-element.4) | data formatting | bytes 262144
  70.2 1.3 %copy.11 = bf16[4,256]{1,0:T(4,128)(2,1)} copy(bf16[4,256]{1,0:T(4,128)(2,1)} %get-tuple-element.5) | data formatting | bytes 4096
